TPU v7x, 256 devices: a whole 4x4x8 slice. The times are simulated.
256 devices in a mesh: space: 128 (over x, y, z), chan: 2 (over core).
Axes of the slice: x: 4, y: 4, z: 8, core: 2. Of those that a mesh axis runs over, the one named last changes fastest.
Arguments:
- features: bfloat16 [262144, 256], P('space', 'chan'), may hold values from -6 to 6
- weights: bfloat16 [27, 256, 256], replicated, may hold values from -0.078125 to 0.078125
- cotangent: bfloat16 [262144, 256], P('space', 'chan'), may hold values from -6 to 6
- pair_offset: int32 [24576], P('space'), may hold values from 0 to 26
- pair_block: int32 [24576], P('space'), may hold values from 0 to 15
- pair_rows: int32 [24576, 128], P('space'), may hold values from 0 to 127
- pair_mask: int32 [24576, 128], P('space'), may hold values 0 or 1
- pair_dest_block: int32 [24576], P('space'), may hold values from 0 to 15
- remote_dest: int32 [16384, 1], P('space'), may hold values from 0 to 127; in each aligned block of 128 rows (0 to 127, 128 to 255, ...) at most 2 rows name the same one
Outputs:
- output: bfloat16 [262144, 256], P('space', 'chan')
- input_grad: bfloat16 [262144, 256], P('space', 'chan')
- weight_grad: float32 [27, 256, 256], P(None, None, 'chan')
Inputs may be any that keep to these rules, and one draw needn't show every extreme that they name: `remote_dest`: among the 128 remote entries of one index of space, no owner is named more than 2 times, and in some indices one owner is named exactly 2 times.
All inputs are finite; a program needn't handle non-finite values. No bound on the sum of `pair_mask` on one device may be relied on, other than what follows from the above.
Results may differ from a plain program's by a relative error of at most 0.009.
Values may be sent and summed in bfloat16 or wider, within the bound.
No kernel may reach another device: no remote copies, remote signals or barrier semaphores. Data moves between devices by JAX's collectives and lax.ppermute only.
A program may use at most 192 MiB of HBM per device.

v0:
```python
import functools

import jax
import jax.numpy as jnp
from jax import lax
from jax.experimental import pallas as pl
from jax.experimental.pallas import tpu as pltpu
from jax.sharding import Mesh
from jax.sharding import PartitionSpec as P

SPACE = ("x", "y", "z")
PLANE = ("x", "y")
SHARES = (11, 13, 16)
FACTORS = {128: (4, 4, 8), 8: (2, 2, 2)}
BF16 = jnp.bfloat16
F32 = jnp.float32

VM = pl.BlockSpec(memory_space=pltpu.VMEM)
SM = pl.BlockSpec(memory_space=pltpu.SMEM)


def pick_transposed(rows_ref, at, block_rows):
    rows = rows_ref[pl.ds(at, 1), :]
    lines = lax.broadcasted_iota(jnp.int32, (block_rows, rows.shape[1]), 0)
    return jnp.where(lines == rows, 1.0, 0.0).astype(BF16)


def forward_block(picked, feats, kernel):
    rows = lax.dot_general(
        picked, feats, (((0,), (0,)), ((), ())), preferred_element_type=F32
    ).astype(BF16)
    return jnp.dot(rows, kernel, preferred_element_type=F32)


def backward_block(picked, upstream, feats_t, kernel, in_ref, block, w_ref, offset):
    spread = jnp.dot(picked, upstream, preferred_element_type=F32).astype(BF16)
    in_ref[block] += lax.dot_general(
        spread, kernel, (((1,), (1,)), ((), ())), preferred_element_type=F32
    )
    w_ref[offset] += jnp.dot(feats_t, spread, preferred_element_type=F32)


def send_kernel(offset, block, rows_ref, feat_ref, kern_ref, out_ref):
    def step(q, carry):
        picked = pick_transposed(rows_ref, q, feat_ref.shape[1])
        out_ref[q] = forward_block(picked, feat_ref[block[q]], kern_ref[offset[q]]).astype(BF16)
        return carry

    lax.fori_loop(0, rows_ref.shape[0], step, 0, unroll=4)


def place_kernel(slot, part_ref, out_ref):
    def step(q, carry):
        out_ref[slot[q]] = part_ref[q]
        return carry

    lax.fori_loop(0, part_ref.shape[0], step, 0, unroll=8)


def pack_kernel(code, cot_ref, out_ref):
    def step(s, carry):
        out_ref[s] = cot_ref[code[s]]
        return carry

    lax.fori_loop(0, out_ref.shape[0], step, 0, unroll=8)


def local_kernel(
    offset, block, dest, rows_ref, feat_ref, feat_t_ref, kern_ref, cot_ref, res_ref, in_ref, w_ref
):
    res_ref[...] = jnp.zeros_like(res_ref)
    in_ref[...] = jnp.zeros_like(in_ref)
    w_ref[...] = jnp.zeros_like(w_ref)

    def step(q, carry):
        b, k, d = block[q], offset[q], dest[q]
        picked = pick_transposed(rows_ref, q, feat_ref.shape[1])
        kernel = kern_ref[k]
        res_ref[d] += forward_block(picked, feat_ref[b], kernel)
        backward_block(picked, cot_ref[d], feat_t_ref[b], kernel, in_ref, b, w_ref, k)
        return carry

    lax.fori_loop(0, rows_ref.shape[0], step, 0)


def remote_kernel(
    offset, block, slot, rows_ref, feat_t_ref, kern_ref, up_ref, in0_ref, w0_ref, in_ref, w_ref
):
    in_ref[...] = in0_ref[...]
    w_ref[...] = w0_ref[...]

    def step(q, carry):
        b, k = block[q], offset[q]
        picked = pick_transposed(rows_ref, q, feat_t_ref.shape[2])
        backward_block(
            picked, up_ref[slot[q]], feat_t_ref[b], kern_ref[k], in_ref, b, w_ref, k
        )
        return carry

    lax.fori_loop(0, rows_ref.shape[0], step, 0, unroll=2)


def column_kernel(code, recv_ref, out_ref, acc_ref):
    acc_ref[...] = jnp.zeros_like(acc_ref)

    def step(s, carry):
        acc_ref[code[s]] += recv_ref[s].astype(F32)
        return carry

    lax.fori_loop(0, recv_ref.shape[0], step, 0, unroll=4)

    def put(b, carry):
        out_ref[b] = acc_ref[b].astype(BF16)
        return carry

    lax.fori_loop(0, out_ref.shape[0], put, 0, unroll=8)


def call(kernel, scalars, arrays, outs, scratch=(), flops=0):
    moved = sum(a.size * a.dtype.itemsize for a in arrays)
    moved += sum(o.size * o.dtype.itemsize for o in outs)
    return pl.pallas_call(
        kernel,
        out_shape=outs,
        in_specs=[SM] * len(scalars) + [VM] * len(arrays),
        out_specs=[VM] * len(outs),
        scratch_shapes=list(scratch),
        cost_estimate=pl.CostEstimate(flops=flops, bytes_accessed=moved, transcendentals=0),
    )(*scalars, *arrays)


def after(a, *others):
    return lax.optimization_barrier((a,) + others)[0]


def axis_exchange(a, axes):
    return lax.all_to_all(a, axes, split_axis=0, concat_axis=0, tiled=True)


def spread(part, axes, count):
    copies = jnp.broadcast_to(part[None], (count,) + part.shape)
    return axis_exchange(copies.reshape((-1,) + part.shape[1:]), axes)


def summed(pieces, count):
    pieces = pieces.reshape((count, -1, pieces.shape[-1]))
    return jnp.sum(pieces.astype(F32), axis=0).astype(BF16)


def spread_weights(pieces, planes, columns):
    part = summed(pieces, planes)
    rows = part.shape[0]
    each = -(-rows // (columns * 16)) * 16
    part = jnp.pad(part, ((0, columns * each - rows), (0, 0)))
    part = summed(axis_exchange(part, "z"), columns)
    return spread(spread(part, "z", columns)[:rows], PLANE, planes)


def body(
    features,
    weights,
    cotangent,
    pair_offset,
    pair_block,
    pair_rows,
    pair_mask,
    pair_dest_block,
    remote_dest,
):
    columns = lax.axis_size("z")
    planes = lax.axis_size("x") * lax.axis_size("y")
    chan = lax.axis_index("chan")
    row_count, width = features.shape
    kernels, in_width, _ = weights.shape
    pair_count, rows = pair_rows.shape
    remote = remote_dest.shape[0]
    local = pair_count - remote
    blocks = row_count // rows
    depth = 2 * columns
    depths = sorted({depth * share // 16 for share in SHARES})

    column_cot = lax.all_gather(cotangent, "z", axis=0, tiled=True)
    column_cot = column_cot.reshape(columns * blocks, rows, width)

    dest = remote_dest[:, 0]
    plane_of = dest // columns
    wanted = (dest % columns) * blocks + pair_dest_block[local:]
    order = jnp.arange(remote, dtype=jnp.int32)
    same = (plane_of[:, None] == plane_of[None, :]) & (order[None, :] < order[:, None])
    rank = jnp.sum(same.astype(jnp.int32), axis=1)
    slot = plane_of * depth + rank
    hits = slot[None, :] == jnp.arange(planes * depth, dtype=jnp.int32)[:, None]
    sent_code = jnp.max(jnp.where(hits, wanted[None, :], -1), axis=1)
    sent_code = jnp.concatenate(
        [sent_code.reshape(planes, depth), jnp.broadcast_to(jnp.max(rank), (planes, 1))], axis=1
    )
    code = axis_exchange(sent_code.reshape(-1), PLANE).reshape(planes, depth + 1)
    most = spread(jnp.max(code[:, depth], keepdims=True), "z", columns)
    code = code[:, :depth]

    picks = jnp.where(pair_mask > 0, pair_rows, rows)
    kern = jnp.where(chan == 0, weights[:, :, :width], weights[:, :, width:])
    other = lax.ppermute(features, "chan", [(0, 1), (1, 0)])
    low = jnp.where(chan == 0, features, other)
    high = jnp.where(chan == 0, other, features)
    feats = jnp.concatenate([low, high], axis=1).reshape(blocks, rows, in_width)
    feats_t = jnp.swapaxes(feats, 1, 2)
    cot_blocks = cotangent.reshape(blocks, rows, width)
    sums = [
        jax.ShapeDtypeStruct((blocks, rows, in_width), F32),
        jax.ShapeDtypeStruct((kernels, in_width, width), F32),
    ]

    parts = call(
        send_kernel,
        (pair_offset[local:], pair_block[local:]),
        (picks[local:], feats, kern),
        [jax.ShapeDtypeStruct((remote, rows, width), BF16)],
        flops=2 * remote * rows * in_width * (rows + width),
    )[0]

    most = jnp.max(after(most, parts))
    tier = jnp.sum((most >= jnp.array(depths[:-1])).astype(jnp.int32))
    grad_scale = (kernels / (pair_count * columns * planes * rows)) ** 0.5

    def exchange(deep):
        slots = planes * deep
        place = plane_of * deep + rank
        codes = code[:, :deep].reshape(slots)
        boxes = [jax.ShapeDtypeStruct((slots, rows, width), BF16)]

        packed = call(pack_kernel, (jnp.maximum(codes, 0),), (column_cot,), boxes)[0]
        upstream = axis_exchange(packed, PLANE)

        resident, in_sum, w_sum = call(
            local_kernel,
            (pair_offset[:local], pair_block[:local], pair_dest_block[:local]),
            (after(picks[:local], packed), feats, feats_t, kern, cot_blocks),
            [jax.ShapeDtypeStruct((blocks, rows, width), F32)] + sums,
            flops=4 * local * rows * in_width * (rows + width),
        )
        placed = call(place_kernel, (place,), (after(parts, packed),), boxes)[0]
        came = axis_exchange(after(placed, upstream, resident), PLANE)

        in_sum, w_sum = call(
            remote_kernel,
            (pair_offset[local:], pair_block[local:], place),
            (picks[local:], feats_t, kern, upstream, in_sum, w_sum),
            sums,
            flops=2 * remote * rows * in_width * (rows + width),
        )
        in_sum = in_sum.reshape(row_count, in_width)
        mine = lax.dynamic_slice_in_dim(in_sum, chan * width, width, 1)
        theirs = lax.dynamic_slice_in_dim(in_sum, (1 - chan) * width, width, 1)
        theirs = lax.ppermute(theirs.astype(BF16), "chan", [(0, 1), (1, 0)])
        input_grad = (mine + theirs.astype(F32)).astype(BF16)

        flat = w_sum.reshape(kernels * in_width, width).astype(BF16)
        pieces = axis_exchange(after(flat, came), PLANE)
        column_sum = call(
            column_kernel,
            (after(jnp.where(codes < 0, columns * blocks, codes), flat, in_sum),),
            (came,),
            [jax.ShapeDtypeStruct((columns * blocks, rows, width), BF16)],
            [pltpu.VMEM((columns * blocks + 1, rows, width), F32)],
        )[0]
        arrived = lax.psum_scatter(column_sum, "z", scatter_dimension=0, tiled=True)
        whole = spread_weights(after(pieces, column_sum), planes, columns)
        weight_grad = (whole.astype(F32) * grad_scale).reshape(kernels, in_width, width)
        output = (resident + arrived.astype(F32)).reshape(row_count, width).astype(BF16)
        return output, input_grad, weight_grad

    return lax.switch(tier, [functools.partial(exchange, deep) for deep in depths])


def solution(mesh):
    x, y, z = FACTORS[mesh.devices.shape[0]]
    split = Mesh(mesh.devices.reshape(x, y, z, -1), SPACE + ("chan",))
    in_specs = (
        P(SPACE, "chan"),
        P(),
        P(SPACE, "chan"),
        P(SPACE),
        P(SPACE),
        P(SPACE, None),
        P(SPACE, None),
        P(SPACE),
        P(SPACE, None),
    )
    out_specs = (P(SPACE, "chan"), P(SPACE, "chan"), P(None, None, "chan"))
    return jax.shard_map(body, mesh=split, in_specs=in_specs, out_specs=out_specs, check_vma=False)
```

profile of v0, /device:TPU:2, one launch (start us, length us, event | category | flops | bytes accessed | tf_op | source)
XLA Modules:
  0.0 353.7 jit_solution(6778006470302288653)
XLA Ops:
  7.3 0.7 all-gather.2.cloned.1.call-update
  8.0 0.7 fusion.4
  8.6 0.8 and_select_fusion.2
  9.6 0.6 fusion.5
  10.4 1.3 concatenate.6
  11.7 7.5 %all-to-all-start.18 = ((s32[16,17,1]{1,2,0:T(1,128)}), s32[16,17,1]{1,2,0:T(1,128)S(1)}, u32[]{:S(2)}, u32[]{:S(2)}) async-start(s32[16,17,1]{1,2,0:T(1,128)} %bitcast.35), calls=%async_computation.21 | async-start | bytes 16384 | tf_op jit(solution)/shard_map/all_to_all | solution.py:137
  19.2 2.2 slice_select_fusion.kern_ref
  21.4 0.6 slice.118.rows_ref
  22.0 0.6 slice.109.offset
  22.6 2.6 all-to-all-done.18
  25.3 0.7 slice_reduce_fusion
  26.0 1.2 reshape.194
  27.2 8.5 %all-to-all-start.19 = ((s32[8,1,1]{2,1,0:T(1,128)}), s32[8,1,1]{2,1,0:T(1,128)S(1)}, u32[]{:S(2)}, u32[]{:S(2)}) async-start(s32[8,1,1]{2,1,0:T(1,128)} %reshape.194), calls=%async_computation.22 | async-start | bytes 8192 | tf_op jit(solution)/shard_map/all_to_all | solution.py:137
  35.7 0.6 slice.110.block
  36.3 7.2 %all-to-all-done.19 = s32[8,1,1]{2,1,0:T(1,128)S(1)} async-done(((s32[8,1,1]{2,1,0:T(1,128)}), s32[8,1,1]{2,1,0:T(1,128)S(1)}, u32[]{:S(2)}, u32[]{:S(2)}) %all-to-all-start.19) | async-done | bytes 64 | tf_op jit(solution)/shard_map/all_to_all | solution.py:137
  44.0 16.6 %shard_map.121 = bf16[128,128,128]{2,1,0:T(8,128)(2,1)} custom-call(s32[128]{0:T(128)} %slice.109.offset, s32[128]{0:T(128)} %slice.110.block, s32[128,128]{1,0:T(8,128)} %slice.118.rows_ref, bf16[16,128,256]{2,1,0:T(8,128)(2,1)S(1)} %bitcast.61, bf16[27,256,128]{2,1,0:T(8,128)(2,1)S(1)} %slice_select_fusion.kern_ref), custom_call_target="tpu_custom_call" | custom-call | flops 2147483648 | bytes 7077888 | tf_op jit(solution)/shard_map/pallas_call | solution.py:122
  60.6 0.6 reduce_max.39
  61.2 1.3 fusion.3
  63.2 4.5 %all-gather.2.cloned.1.call-done = bf16[16384,128]{1,0:T(8,128)(2,1)} async-done(((bf16[2048,128]{1,0:T(8,128)(2,1)}), bf16[16384,128]{1,0:T(8,128)(2,1)}) %all-gather.2.cloned.1.call-update) | async-done | bytes 4194320 | tf_op jit(solution)/shard_map/all_gather | solution.py:182
  67.6 278.2 %conditional.4 = (f32[27,256,128]{2,1,0:T(8,128)}, bf16[2048,128]{1,0:T(8,128)(2,1)S(1)}, bf16[2048,128]{1,0:T(8,128)(2,1)S(1)}) conditional(s32[]{:T(128)} %clamp.3, (s32[192]{0:T(256)S(1)}, s32[192]{0:T(256)S(1)}, s32[128]{0:T(128)S(1)}, s32[128]{0:T(128)S(1)}, s32[192,128]{1,0:T(8,128)S(1)}, ...), branch_computations={%region_6.10_spmd, %region_10.14_spmd, %region_14.18_spmd} | conditional | flops 4300082176 | bytes 174233984
  67.7 0.6 compare_select_fusion
  68.3 5.1 %branch_0_fun.5 = bf16[176,128,128]{2,1,0:T(8,128)(2,1)} custom-call(s32[176]{0:T(256)} %get-tuple-element.367.code, bf16[128,128,128]{2,1,0:T(8,128)(2,1)} %bitcast.58), custom_call_target="tpu_custom_call" | custom-call | bytes 9961472 | tf_op jit(solution)/shard_map/cond/branch_0_fun/pallas_call | solution.py:122
  73.4 7.3 %all-to-all-start = ((bf16[176,128,128]{2,1,0:T(8,128)(2,1)}), bf16[176,128,128]{2,1,0:T(8,128)(2,1)}, u32[]{:S(2)}, u32[]{:S(2)}) async-start(bf16[176,128,128]{2,1,0:T(8,128)(2,1)} %branch_0_fun.5), calls=%async_computation | async-start | bytes 11534336 | tf_op jit(solution)/shard_map/cond/branch_0_fun/all_to_all | solution.py:137
  80.7 0.6 slice.80.rows_ref
  81.3 1.3 copy.22.feat_t_ref
  84.2 0.6 multiply_add_fusion.slot
  84.8 5.1 %branch_0_fun.8 = bf16[176,128,128]{2,1,0:T(8,128)(2,1)} custom-call(s32[128]{0:T(128)} %multiply_add_fusion.slot, bf16[128,128,128]{2,1,0:T(8,128)(2,1)} %get-tuple-element.124.part_ref), custom_call_target="tpu_custom_call" | custom-call | bytes 9961472 | tf_op jit(solution)/shard_map/cond/branch_0_fun/pallas_call | solution.py:122
  89.9 28.2 %branch_0_fun.6 = (f32[16,128,128]{2,1,0:T(8,128)}, f32[16,128,256]{2,1,0:T(8,128)}, f32[27,256,128]{2,1,0:T(8,128)}) custom-call(s32[64]{0:T(128)} %slice.77.offset, s32[64]{0:T(128)} %slice.78.block, s32[64]{0:T(128)} %slice.79.dest, s32[64,128]{1,0:T(8,128)} %slice.80.rows_ref, bf16[16,128,256]{2,1,0:T(8,128)(2,1)S(1)} %bitcast.68, ...), custom_call_target="tpu_custom_call" | custom-call | flops 2147483648 | bytes 11108352 | tf_op jit(solution)/shard_map/cond/branch_0_fun/pallas_call | solution.py:122
  118.1 35.6 %all-to-all-done.up_ref = bf16[176,128,128]{2,1,0:T(8,128)(2,1)} async-done(((bf16[176,128,128]{2,1,0:T(8,128)(2,1)}), bf16[176,128,128]{2,1,0:T(8,128)(2,1)}, u32[]{:S(2)}, u32[]{:S(2)}) %all-to-all-start) | async-done | bytes 5767200 | tf_op jit(solution)/shard_map/cond/branch_0_fun/all_to_all | solution.py:137
  153.7 28.5 %all-to-all-start.1 = ((bf16[176,128,128]{2,1,0:T(8,128)(2,1)}), bf16[176,128,128]{2,1,0:T(8,128)(2,1)}, u32[]{:S(2)}, u32[]{:S(2)}) async-start(bf16[176,128,128]{2,1,0:T(8,128)(2,1)} %branch_0_fun.8), calls=%async_computation.1 | async-start | bytes 11534336 | tf_op jit(solution)/shard_map/cond/branch_0_fun/all_to_all | solution.py:137
  182.2 0.6 slice.75.rows_ref
  182.8 0.6 slice.73.offset
  184.0 37.7 %branch_0_fun.7 = (f32[16,128,256]{2,1,0:T(8,128)}, f32[27,256,128]{2,1,0:T(8,128)}) custom-call(s32[128]{0:T(128)} %slice.73.offset, s32[128]{0:T(128)} %slice.74.block, s32[128]{0:T(128)} %multiply_add_fusion.slot, s32[128,128]{1,0:T(8,128)} %slice.75.rows_ref, bf16[16,256,128]{2,1,0:T(8,128)(2,1)} %copy.22.feat_t_ref, ...), custom_call_target="tpu_custom_call" | custom-call | flops 2147483648 | bytes 19922944 | tf_op jit(solution)/shard_map/cond/branch_0_fun/pallas_call | solution.py:122
  221.7 2.3 convert_element_type.96
  224.0 28.4 %all-to-all-done.1.recv_ref = bf16[176,128,128]{2,1,0:T(8,128)(2,1)} async-done(((bf16[176,128,128]{2,1,0:T(8,128)(2,1)}), bf16[176,128,128]{2,1,0:T(8,128)(2,1)}, u32[]{:S(2)}, u32[]{:S(2)}) %all-to-all-start.1) | async-done | bytes 5767200 | tf_op jit(solution)/shard_map/cond/branch_0_fun/all_to_all | solution.py:137
  252.4 7.0 %branch_0_fun.9 = bf16[128,128,128]{2,1,0:T(8,128)(2,1)} custom-call(s32[176]{0:T(256)} %get-tuple-element.129.code, bf16[176,128,128]{2,1,0:T(8,128)(2,1)} %all-to-all-done.1.recv_ref), custom_call_target="tpu_custom_call" | custom-call | bytes 9961472 | tf_op jit(solution)/shard_map/cond/branch_0_fun/pallas_call | solution.py:122
  259.4 32.1 %all_to_all.126 = bf16[16,432,128]{2,1,0:T(8,128)(2,1)S(1)} all-to-all(bf16[16,432,128]{2,1,0:T(8,128)(2,1)S(1)} %bitcast.71), channel_id=1, replica_groups=mesh['x'=4,'y'=4,'z'=8,'chan'=2] {'x','y'}, dimensions={0} | all-to-all | bytes 3538944 | tf_op jit(solution)/shard_map/cond/branch_0_fun/all_to_all | solution.py:137
  291.8 14.8 %all_to_all.127 = bf16[8,64,128]{2,1,0:T(8,128)(2,1)S(1)} all-to-all(bf16[8,64,128]{2,1,0:T(8,128)(2,1)S(1)} %bitcast.86), channel_id=1, replica_groups=mesh['x'=4,'y'=4,'z'=8,'chan'=2] {'z'}, dimensions={0} | all-to-all | bytes 262144 | tf_op jit(solution)/shard_map/cond/branch_0_fun/all_to_all | solution.py:137
  306.6 13.0 %all_to_all.128 = bf16[8,64,128]{2,1,0:T(8,128)(2,1)S(1)} all-to-all(bf16[8,64,128]{2,1,0:T(8,128)(2,1)S(1)} %broadcast_in_dim.27), channel_id=1, replica_groups=mesh['x'=4,'y'=4,'z'=8,'chan'=2] {'z'}, dimensions={0} | all-to-all | bytes 262144 | tf_op jit(solution)/shard_map/cond/branch_0_fun/all_to_all | solution.py:137
  319.6 1.4 broadcast_in_dim.28
  321.0 5.3 %all-to-all-start.5 = ((bf16[16,432,128]{2,1,0:T(8,128)(2,1)}), bf16[16,432,128]{2,1,0:T(8,128)(2,1)S(1)}, u32[]{:S(2)}, u32[]{:S(2)}) async-start(bf16[16,432,128]{2,1,0:T(8,128)(2,1)} %broadcast_in_dim.28), calls=%async_computation.5 | async-start | bytes 3538944 | tf_op jit(solution)/shard_map/cond/branch_0_fun/all_to_all | solution.py:137
  326.3 1.3 dynamic-slice_convert_fusion
  327.7 2.0 collective-permute-done
  329.7 1.5 add_convert_fusion.1
  331.2 11.2 %all-to-all-done.5 = bf16[16,432,128]{2,1,0:T(8,128)(2,1)S(1)} async-done(((bf16[16,432,128]{2,1,0:T(8,128)(2,1)}), bf16[16,432,128]{2,1,0:T(8,128)(2,1)S(1)}, u32[]{:S(2)}, u32[]{:S(2)}) %all-to-all-start.5) | async-done | bytes 1769504 | tf_op jit(solution)/shard_map/cond/branch_0_fun/all_to_all | solution.py:137
  342.4 2.0 convert_multiply_fusion
  344.5 1.2 add_convert_fusion
  345.9 0.8 copy-done.4
  (45 shorter events, 3.7 us)
Async XLA Ops:
  7.2 36.6 %copy-start.3 = (bf16[2048,128]{1,0:T(8,128)(2,1)S(1)}, bf16[2048,128]{1,0:T(8,128)(2,1)}, u32[]{:S(2)}) copy-start(bf16[2048,128]{1,0:T(8,128)(2,1)} %param.13) | copy-start | bytes 1572868
  7.2 14.2 %copy-start.7 = (s32[192,128]{1,0:T(8,128)S(1)}, s32[192,128]{1,0:T(8,128)}, u32[]{:S(2)}) copy-start(s32[192,128]{1,0:T(8,128)} %param.18) | copy-start | bytes 294916
  7.2 14.2 %copy-start.8 = (s32[192,128]{1,0:T(8,128)S(1)}, s32[192,128]{1,0:T(8,128)}, u32[]{:S(2)}) copy-start(s32[192,128]{1,0:T(8,128)} %param.19) | copy-start | bytes 294916
  7.2 14.8 %copy-start.10 = (s32[192]{0:T(256)S(1)}, s32[192]{0:T(256)}, u32[]{:S(2)}) copy-start(s32[192]{0:T(256)} %param.16) | copy-start | bytes 2308
  7.2 28.5 %copy-start.11 = (s32[192]{0:T(256)S(1)}, s32[192]{0:T(256)}, u32[]{:S(2)}) copy-start(s32[192]{0:T(256)} %param.17) | copy-start | bytes 2308
  7.2 60.4 %all-gather.2.cloned.1.call-start = ((), (), s32[]{:S(2)}) async-start(), calls=%async_computation.26 | async-start | bytes 4718592 | tf_op jit(solution)/shard_map/all_gather | solution.py:182
  11.7 13.6 %all-to-all-start.18 = ((s32[16,17,1]{1,2,0:T(1,128)}), s32[16,17,1]{1,2,0:T(1,128)S(1)}, u32[]{:S(2)}, u32[]{:S(2)}) async-start(s32[16,17,1]{1,2,0:T(1,128)} %bitcast.35), calls=%async_computation.21 | async-start | bytes 16384 | tf_op jit(solution)/shard_map/all_to_all | solution.py:137
  19.1 24.6 %collective-permute-start.3 = (bf16[2048,128]{1,0:T(8,128)(2,1)}, bf16[2048,128]{1,0:T(8,128)(2,1)S(1)}, u32[]{:S(2)}, u32[]{:S(2)}) collective-permute-start(bf16[2048,128]{1,0:T(8,128)(2,1)} %param.13), channel_id=1, source_target_pairs={{0,1},{1,0},{2,3},{3,2},{4,5},{5,4},{6,7},{7,6},{8,9},{9,8},{10,11... | collective-permute-start | bytes 1572872 | tf_op jit(solution)/shard_map/ppermute | solution.py:203
  27.2 16.3 %all-to-all-start.19 = ((s32[8,1,1]{2,1,0:T(1,128)}), s32[8,1,1]{2,1,0:T(1,128)S(1)}, u32[]{:S(2)}, u32[]{:S(2)}) async-start(s32[8,1,1]{2,1,0:T(1,128)} %reshape.194), calls=%async_computation.22 | async-start | bytes 8192 | tf_op jit(solution)/shard_map/all_to_all | solution.py:137
  44.0 17.3 %copy-start.12 = (s32[2]{0:T(128)S(1)}, s32[2]{0:T(128)}, u32[]{:S(2)}) copy-start(s32[2]{0:T(128)} %constant.99.clone) | copy-start | bytes 28
  44.0 23.7 %copy-start.5 = (bf16[2048,128]{1,0:T(8,128)(2,1)S(1)}, bf16[2048,128]{1,0:T(8,128)(2,1)}, u32[]{:S(2)}) copy-start(bf16[2048,128]{1,0:T(8,128)(2,1)} %param.15) | copy-start | bytes 1572868
  44.0 23.7 %copy-start.9 = (s32[192]{0:T(256)S(1)}, s32[192]{0:T(256)}, u32[]{:S(2)}) copy-start(s32[192]{0:T(256)} %param.20) | copy-start | bytes 2308
  73.4 80.2 %all-to-all-start = ((bf16[176,128,128]{2,1,0:T(8,128)(2,1)}), bf16[176,128,128]{2,1,0:T(8,128)(2,1)}, u32[]{:S(2)}, u32[]{:S(2)}) async-start(bf16[176,128,128]{2,1,0:T(8,128)(2,1)} %branch_0_fun.5), calls=%async_computation | async-start | bytes 11534336 | tf_op jit(solution)/shard_map/cond/branch_0_fun/all_to_all | solution.py:137
  153.7 98.7 %all-to-all-start.1 = ((bf16[176,128,128]{2,1,0:T(8,128)(2,1)}), bf16[176,128,128]{2,1,0:T(8,128)(2,1)}, u32[]{:S(2)}, u32[]{:S(2)}) async-start(bf16[176,128,128]{2,1,0:T(8,128)(2,1)} %branch_0_fun.8), calls=%async_computation.1 | async-start | bytes 11534336 | tf_op jit(solution)/shard_map/cond/branch_0_fun/all_to_all | solution.py:137
  182.2 162.3 %reduce-scatter.4.cloned.1.call-start = ((), (), s32[]{:S(2)}) async-start(), calls=%async_computation.23 | async-start | bytes 4718592 | tf_op jit(solution)/shard_map/cond/branch_0_fun/reduce_scatter | solution.py:267
  321.0 21.4 %all-to-all-start.5 = ((bf16[16,432,128]{2,1,0:T(8,128)(2,1)}), bf16[16,432,128]{2,1,0:T(8,128)(2,1)S(1)}, u32[]{:S(2)}, u32[]{:S(2)}) async-start(bf16[16,432,128]{2,1,0:T(8,128)(2,1)} %broadcast_in_dim.28), calls=%async_computation.5 | async-start | bytes 3538944 | tf_op jit(solution)/shard_map/cond/branch_0_fun/all_to_all | solution.py:137
  327.6 2.1 collective-permute-start
  327.7 16.8 %copy-start = (f32[16,128,128]{2,1,0:T(8,128)S(1)}, f32[16,128,128]{2,1,0:T(8,128)}, u32[]{:S(2)}) copy-start(f32[16,128,128]{2,1,0:T(8,128)} %get-tuple-element.125) | copy-start | bytes 3145732
  345.9 0.8 copy-start.4
  345.9 1.0 copy-start.6
Sparse Core Ops, SparseCore 0:
  9.8 57.7 all-gather.1
  259.5 66.5 reduce-scatter.3
where the time goes:
time: 355 us; the launch traced here: 354 us
  Pallas kernels  99.7 us (28%)
  waiting for transfers between devices  92.3 us (26%)
  blocking collectives  59.9 us (17%)
  starting transfers between devices  57.1 us (16%)
  other arithmetic  16 us (5%)
  between operations  14.9 us (4%)
  local copies, waits for them, and re-layouts  13.5 us (4%)
    pallas_call x6, Pallas kernels, call(): pl.pallas_call(kernel, out_shape=outs, in_specs=[SM] * len(scalars) + [VM...  99.7 us
    all_to_all x5, waiting for transfers between devices, axis_exchange(): return lax.all_to_all(a, axes, split_axis=0, concat_axis=0, tiled=True)  85.1 us
    all_to_all x3, blocking collectives, axis_exchange(): return lax.all_to_all(a, axes, split_axis=0, concat_axis=0, tiled=True)  59.9 us
    all_to_all x5, starting transfers between devices, axis_exchange(): return lax.all_to_all(a, axes, split_axis=0, concat_axis=0, tiled=True)  56.9 us
  transfers between devices with their start and end apart: 9, of which 7 were waited for; matrix products, arithmetic and copies ran while one was open for 8% of the time, Pallas kernels for 25%

commit v1 on v0

--- a/solution.py
+++ b/solution.py
@@ -80,7 +80,7 @@
         backward_block(picked, cot_ref[d], feat_t_ref[b], kernel, in_ref, b, w_ref, k)
         return carry
 
-    lax.fori_loop(0, rows_ref.shape[0], step, 0)
+    lax.fori_loop(0, rows_ref.shape[0], step, 0, unroll=2)
 
 
 def remote_kernel(
@@ -97,7 +97,7 @@
         )
         return carry
 
-    lax.fori_loop(0, rows_ref.shape[0], step, 0, unroll=2)
+    lax.fori_loop(0, rows_ref.shape[0], step, 0, unroll=4)
 
 
 def column_kernel(code, recv_ref, out_ref, acc_ref):
@@ -235,12 +235,12 @@
         resident, in_sum, w_sum = call(
             local_kernel,
             (pair_offset[:local], pair_block[:local], pair_dest_block[:local]),
-            (after(picks[:local], packed), feats, feats_t, kern, cot_blocks),
+            (after(picks[:local], upstream), feats, feats_t, kern, cot_blocks),
             [jax.ShapeDtypeStruct((blocks, rows, width), F32)] + sums,
             flops=4 * local * rows * in_width * (rows + width),
         )
         placed = call(place_kernel, (place,), (after(parts, packed),), boxes)[0]
-        came = axis_exchange(after(placed, upstream, resident), PLANE)
+        came = axis_exchange(after(placed, upstream), PLANE)
 
         in_sum, w_sum = call(
             remote_kernel,

time: 355 us -> 355 us (level)
  waiting for transfers between devices: 92.3 us -> 103 us
  Pallas kernels: 99.7 us -> 89.2 us
    all_to_all x5, waiting for transfers between devices: 85.1 us -> 95.8 us  [axis_exchange(): return lax.all_to_all(a, axes, split_axis=0, concat_axis=0, tiled=True)]
    pallas_call x6, Pallas kernels: 99.7 us -> 89.2 us  [call(): pl.pallas_call(kernel, out_shape=outs, in_specs=[SM] * len(scalars) + [VM...]
  transfers between devices with their start and end apart: 9 -> 9, of which waited for: 7 -> 7; matrix products, arithmetic and copies ran while one was open for 8% -> 8% of each run, Pallas kernels for 25% -> 22%
where the time goes in v1:
time: 355 us; the launch traced here: 354 us
  waiting for transfers between devices  103 us (29%)
  Pallas kernels  89.2 us (25%)
  blocking collectives  59.9 us (17%)
  starting transfers between devices  57.1 us (16%)
  other arithmetic  16 us (5%)
  between operations  14.9 us (4%)
  local copies, waits for them, and re-layouts  13.5 us (4%)
    all_to_all x5, waiting for transfers between devices, axis_exchange(): return lax.all_to_all(a, axes, split_axis=0, concat_axis=0, tiled=True)  95.8 us
    pallas_call x6, Pallas kernels, call(): pl.pallas_call(kernel, out_shape=outs, in_specs=[SM] * len(scalars) + [VM...  89.2 us
    all_to_all x3, blocking collectives, axis_exchange(): return lax.all_to_all(a, axes, split_axis=0, concat_axis=0, tiled=True)  59.9 us
    all_to_all x5, starting transfers between devices, axis_exchange(): return lax.all_to_all(a, axes, split_axis=0, concat_axis=0, tiled=True)  56.9 us
  transfers between devices with their start and end apart: 9, of which 7 were waited for; matrix products, arithmetic and copies ran while one was open for 8% of the time, Pallas kernels for 22%

profile of v1, /device:TPU:2, one launch (start us, length us, event | category | flops | bytes accessed | tf_op | source)
XLA Modules:
  0.0 353.8 jit_solution(1947531728242084548)
XLA Ops:
  7.3 0.7 all-gather.2.cloned.1.call-update
  8.0 0.7 fusion.4
  8.6 0.8 and_select_fusion.2
  9.6 0.6 fusion.5
  10.4 1.3 concatenate.6
  11.7 7.5 %all-to-all-start.18 = ((s32[16,17,1]{1,2,0:T(1,128)}), s32[16,17,1]{1,2,0:T(1,128)S(1)}, u32[]{:S(2)}, u32[]{:S(2)}) async-start(s32[16,17,1]{1,2,0:T(1,128)} %bitcast.35), calls=%async_computation.21 | async-start | bytes 16384 | tf_op jit(solution)/shard_map/all_to_all | solution.py:137
  19.2 2.2 slice_select_fusion.kern_ref
  21.4 0.6 slice.118.rows_ref
  22.0 0.6 slice.109.offset
  22.6 2.6 all-to-all-done.18
  25.3 0.7 slice_reduce_fusion
  26.0 1.2 reshape.194
  27.2 8.5 %all-to-all-start.19 = ((s32[8,1,1]{2,1,0:T(1,128)}), s32[8,1,1]{2,1,0:T(1,128)S(1)}, u32[]{:S(2)}, u32[]{:S(2)}) async-start(s32[8,1,1]{2,1,0:T(1,128)} %reshape.194), calls=%async_computation.22 | async-start | bytes 8192 | tf_op jit(solution)/shard_map/all_to_all | solution.py:137
  35.7 0.6 slice.110.block
  36.3 7.2 %all-to-all-done.19 = s32[8,1,1]{2,1,0:T(1,128)S(1)} async-done(((s32[8,1,1]{2,1,0:T(1,128)}), s32[8,1,1]{2,1,0:T(1,128)S(1)}, u32[]{:S(2)}, u32[]{:S(2)}) %all-to-all-start.19) | async-done | bytes 64 | tf_op jit(solution)/shard_map/all_to_all | solution.py:137
  44.0 16.6 %shard_map.121 = bf16[128,128,128]{2,1,0:T(8,128)(2,1)} custom-call(s32[128]{0:T(128)} %slice.109.offset, s32[128]{0:T(128)} %slice.110.block, s32[128,128]{1,0:T(8,128)} %slice.118.rows_ref, bf16[16,128,256]{2,1,0:T(8,128)(2,1)S(1)} %bitcast.61, bf16[27,256,128]{2,1,0:T(8,128)(2,1)S(1)} %slice_select_fusion.kern_ref), custom_call_target="tpu_custom_call" | custom-call | flops 2147483648 | bytes 7077888 | tf_op jit(solution)/shard_map/pallas_call | solution.py:122
  60.6 0.6 reduce_max.39
  61.2 1.3 fusion.3
  63.2 4.5 %all-gather.2.cloned.1.call-done = bf16[16384,128]{1,0:T(8,128)(2,1)} async-done(((bf16[2048,128]{1,0:T(8,128)(2,1)}), bf16[16384,128]{1,0:T(8,128)(2,1)}) %all-gather.2.cloned.1.call-update) | async-done | bytes 4194320 | tf_op jit(solution)/shard_map/all_gather | solution.py:182
  67.6 278.3 %conditional.4 = (f32[27,256,128]{2,1,0:T(8,128)}, bf16[2048,128]{1,0:T(8,128)(2,1)S(1)}, bf16[2048,128]{1,0:T(8,128)(2,1)S(1)}) conditional(s32[]{:T(128)} %clamp.3, (s32[192]{0:T(256)S(1)}, s32[192]{0:T(256)S(1)}, s32[128]{0:T(128)S(1)}, s32[128]{0:T(128)S(1)}, s32[192,128]{1,0:T(8,128)S(1)}, ...), branch_computations={%region_6.10_spmd, %region_10.14_spmd, %region_14.18_spmd} | conditional | flops 4300082176 | bytes 174233984
  67.7 0.6 compare_select_fusion
  68.3 5.2 %branch_0_fun.5 = bf16[176,128,128]{2,1,0:T(8,128)(2,1)} custom-call(s32[176]{0:T(256)} %get-tuple-element.367.code, bf16[128,128,128]{2,1,0:T(8,128)(2,1)} %bitcast.58), custom_call_target="tpu_custom_call" | custom-call | bytes 9961472 | tf_op jit(solution)/shard_map/cond/branch_0_fun/pallas_call | solution.py:122
  73.5 7.3 %all-to-all-start = ((bf16[176,128,128]{2,1,0:T(8,128)(2,1)}), bf16[176,128,128]{2,1,0:T(8,128)(2,1)}, u32[]{:S(2)}, u32[]{:S(2)}) async-start(bf16[176,128,128]{2,1,0:T(8,128)(2,1)} %branch_0_fun.5), calls=%async_computation | async-start | bytes 11534336 | tf_op jit(solution)/shard_map/cond/branch_0_fun/all_to_all | solution.py:137
  81.3 5.1 %branch_0_fun.8 = bf16[176,128,128]{2,1,0:T(8,128)(2,1)} custom-call(s32[128]{0:T(128)} %multiply_add_fusion.slot, bf16[128,128,128]{2,1,0:T(8,128)(2,1)} %get-tuple-element.124.part_ref), custom_call_target="tpu_custom_call" | custom-call | bytes 9961472 | tf_op jit(solution)/shard_map/cond/branch_0_fun/pallas_call | solution.py:122
  86.4 67.3 %all-to-all-done.up_ref = bf16[176,128,128]{2,1,0:T(8,128)(2,1)} async-done(((bf16[176,128,128]{2,1,0:T(8,128)(2,1)}), bf16[176,128,128]{2,1,0:T(8,128)(2,1)}, u32[]{:S(2)}, u32[]{:S(2)}) %all-to-all-start) | async-done | bytes 5767200 | tf_op jit(solution)/shard_map/cond/branch_0_fun/all_to_all | solution.py:137
  153.8 28.5 %all-to-all-start.1 = ((bf16[176,128,128]{2,1,0:T(8,128)(2,1)}), bf16[176,128,128]{2,1,0:T(8,128)(2,1)}, u32[]{:S(2)}, u32[]{:S(2)}) async-start(bf16[176,128,128]{2,1,0:T(8,128)(2,1)} %branch_0_fun.8), calls=%async_computation.1 | async-start | bytes 11534336 | tf_op jit(solution)/shard_map/cond/branch_0_fun/all_to_all | solution.py:137
  182.3 0.6 slice.80.rows_ref
  182.9 0.6 slice.75.rows_ref
  184.0 0.6 slice.73.offset
  185.1 0.6 slice.74.block
  185.8 1.3 copy.22.feat_t_ref
  187.6 22.6 %branch_0_fun.6 = (f32[16,128,128]{2,1,0:T(8,128)}, f32[16,128,256]{2,1,0:T(8,128)}, f32[27,256,128]{2,1,0:T(8,128)}) custom-call(s32[64]{0:T(128)} %slice.77.offset, s32[64]{0:T(128)} %slice.78.block, s32[64]{0:T(128)} %slice.79.dest, s32[64,128]{1,0:T(8,128)} %slice.80.rows_ref, bf16[16,128,256]{2,1,0:T(8,128)(2,1)S(1)} %bitcast.68, ...), custom_call_target="tpu_custom_call" | custom-call | flops 2147483648 | bytes 11108352 | tf_op jit(solution)/shard_map/cond/branch_0_fun/pallas_call | solution.py:122
  210.1 32.7 %branch_0_fun.7 = (f32[16,128,256]{2,1,0:T(8,128)}, f32[27,256,128]{2,1,0:T(8,128)}) custom-call(s32[128]{0:T(128)} %slice.73.offset, s32[128]{0:T(128)} %slice.74.block, s32[128]{0:T(128)} %multiply_add_fusion.slot, s32[128,128]{1,0:T(8,128)} %slice.75.rows_ref, bf16[16,256,128]{2,1,0:T(8,128)(2,1)} %copy.22.feat_t_ref, ...), custom_call_target="tpu_custom_call" | custom-call | flops 2147483648 | bytes 19922944 | tf_op jit(solution)/shard_map/cond/branch_0_fun/pallas_call | solution.py:122
  242.8 2.3 convert_element_type.96
  245.1 7.3 %all-to-all-done.1.recv_ref = bf16[176,128,128]{2,1,0:T(8,128)(2,1)} async-done(((bf16[176,128,128]{2,1,0:T(8,128)(2,1)}), bf16[176,128,128]{2,1,0:T(8,128)(2,1)}, u32[]{:S(2)}, u32[]{:S(2)}) %all-to-all-start.1) | async-done | bytes 5767200 | tf_op jit(solution)/shard_map/cond/branch_0_fun/all_to_all | solution.py:137
  252.5 7.0 %branch_0_fun.9 = bf16[128,128,128]{2,1,0:T(8,128)(2,1)} custom-call(s32[176]{0:T(256)} %get-tuple-element.128.code, bf16[176,128,128]{2,1,0:T(8,128)(2,1)} %all-to-all-done.1.recv_ref), custom_call_target="tpu_custom_call" | custom-call | bytes 9961472 | tf_op jit(solution)/shard_map/cond/branch_0_fun/pallas_call | solution.py:122
  259.5 32.1 %all_to_all.126 = bf16[16,432,128]{2,1,0:T(8,128)(2,1)S(1)} all-to-all(bf16[16,432,128]{2,1,0:T(8,128)(2,1)S(1)} %bitcast.71), channel_id=1, replica_groups=mesh['x'=4,'y'=4,'z'=8,'chan'=2] {'x','y'}, dimensions={0} | all-to-all | bytes 3538944 | tf_op jit(solution)/shard_map/cond/branch_0_fun/all_to_all | solution.py:137
  291.9 14.7 %all_to_all.127 = bf16[8,64,128]{2,1,0:T(8,128)(2,1)S(1)} all-to-all(bf16[8,64,128]{2,1,0:T(8,128)(2,1)S(1)} %bitcast.86), channel_id=1, replica_groups=mesh['x'=4,'y'=4,'z'=8,'chan'=2] {'z'}, dimensions={0} | all-to-all | bytes 262144 | tf_op jit(solution)/shard_map/cond/branch_0_fun/all_to_all | solution.py:137
  306.7 13.0 %all_to_all.128 = bf16[8,64,128]{2,1,0:T(8,128)(2,1)S(1)} all-to-all(bf16[8,64,128]{2,1,0:T(8,128)(2,1)S(1)} %broadcast_in_dim.27), channel_id=1, replica_groups=mesh['x'=4,'y'=4,'z'=8,'chan'=2] {'z'}, dimensions={0} | all-to-all | bytes 262144 | tf_op jit(solution)/shard_map/cond/branch_0_fun/all_to_all | solution.py:137
  319.7 1.4 broadcast_in_dim.28
  321.2 5.2 %all-to-all-start.5 = ((bf16[16,432,128]{2,1,0:T(8,128)(2,1)}), bf16[16,432,128]{2,1,0:T(8,128)(2,1)S(1)}, u32[]{:S(2)}, u32[]{:S(2)}) async-start(bf16[16,432,128]{2,1,0:T(8,128)(2,1)} %broadcast_in_dim.28), calls=%async_computation.5 | async-start | bytes 3538944 | tf_op jit(solution)/shard_map/cond/branch_0_fun/all_to_all | solution.py:137
  326.4 1.3 dynamic-slice_convert_fusion
  327.8 2.0 collective-permute-done
  329.8 1.5 add_convert_fusion.1
  331.3 11.2 %all-to-all-done.5 = bf16[16,432,128]{2,1,0:T(8,128)(2,1)S(1)} async-done(((bf16[16,432,128]{2,1,0:T(8,128)(2,1)}), bf16[16,432,128]{2,1,0:T(8,128)(2,1)S(1)}, u32[]{:S(2)}, u32[]{:S(2)}) %all-to-all-start.5) | async-done | bytes 1769504 | tf_op jit(solution)/shard_map/cond/branch_0_fun/all_to_all | solution.py:137
  342.5 2.0 convert_multiply_fusion
  344.6 1.2 add_convert_fusion
  346.0 0.8 copy-done.4
  (45 shorter events, 3.6 us)
Async XLA Ops:
  7.2 36.6 %copy-start.3 = (bf16[2048,128]{1,0:T(8,128)(2,1)S(1)}, bf16[2048,128]{1,0:T(8,128)(2,1)}, u32[]{:S(2)}) copy-start(bf16[2048,128]{1,0:T(8,128)(2,1)} %param.13) | copy-start | bytes 1572868
  7.2 14.2 %copy-start.7 = (s32[192,128]{1,0:T(8,128)S(1)}, s32[192,128]{1,0:T(8,128)}, u32[]{:S(2)}) copy-start(s32[192,128]{1,0:T(8,128)} %param.18) | copy-start | bytes 294916
  7.2 14.2 %copy-start.8 = (s32[192,128]{1,0:T(8,128)S(1)}, s32[192,128]{1,0:T(8,128)}, u32[]{:S(2)}) copy-start(s32[192,128]{1,0:T(8,128)} %param.19) | copy-start | bytes 294916
  7.2 14.8 %copy-start.10 = (s32[192]{0:T(256)S(1)}, s32[192]{0:T(256)}, u32[]{:S(2)}) copy-start(s32[192]{0:T(256)} %param.16) | copy-start | bytes 2308
  7.2 28.5 %copy-start.11 = (s32[192]{0:T(256)S(1)}, s32[192]{0:T(256)}, u32[]{:S(2)}) copy-start(s32[192]{0:T(256)} %param.17) | copy-start | bytes 2308
  7.2 60.4 %all-gather.2.cloned.1.call-start = ((), (), s32[]{:S(2)}) async-start(), calls=%async_computation.26 | async-start | bytes 4718592 | tf_op jit(solution)/shard_map/all_gather | solution.py:182
  11.7 13.6 %all-to-all-start.18 = ((s32[16,17,1]{1,2,0:T(1,128)}), s32[16,17,1]{1,2,0:T(1,128)S(1)}, u32[]{:S(2)}, u32[]{:S(2)}) async-start(s32[16,17,1]{1,2,0:T(1,128)} %bitcast.35), calls=%async_computation.21 | async-start | bytes 16384 | tf_op jit(solution)/shard_map/all_to_all | solution.py:137
  19.1 24.6 %collective-permute-start.3 = (bf16[2048,128]{1,0:T(8,128)(2,1)}, bf16[2048,128]{1,0:T(8,128)(2,1)S(1)}, u32[]{:S(2)}, u32[]{:S(2)}) collective-permute-start(bf16[2048,128]{1,0:T(8,128)(2,1)} %param.13), channel_id=1, source_target_pairs={{0,1},{1,0},{2,3},{3,2},{4,5},{5,4},{6,7},{7,6},{8,9},{9,8},{10,11... | collective-permute-start | bytes 1572872 | tf_op jit(solution)/shard_map/ppermute | solution.py:203
  27.2 16.3 %all-to-all-start.19 = ((s32[8,1,1]{2,1,0:T(1,128)}), s32[8,1,1]{2,1,0:T(1,128)S(1)}, u32[]{:S(2)}, u32[]{:S(2)}) async-start(s32[8,1,1]{2,1,0:T(1,128)} %reshape.194), calls=%async_computation.22 | async-start | bytes 8192 | tf_op jit(solution)/shard_map/all_to_all | solution.py:137
  44.0 17.3 %copy-start.12 = (s32[2]{0:T(128)S(1)}, s32[2]{0:T(128)}, u32[]{:S(2)}) copy-start(s32[2]{0:T(128)} %constant.99.clone) | copy-start | bytes 28
  44.0 23.7 %copy-start.5 = (bf16[2048,128]{1,0:T(8,128)(2,1)S(1)}, bf16[2048,128]{1,0:T(8,128)(2,1)}, u32[]{:S(2)}) copy-start(bf16[2048,128]{1,0:T(8,128)(2,1)} %param.15) | copy-start | bytes 1572868
  44.0 23.7 %copy-start.9 = (s32[192]{0:T(256)S(1)}, s32[192]{0:T(256)}, u32[]{:S(2)}) copy-start(s32[192]{0:T(256)} %param.20) | copy-start | bytes 2308
  73.5 80.2 %all-to-all-start = ((bf16[176,128,128]{2,1,0:T(8,128)(2,1)}), bf16[176,128,128]{2,1,0:T(8,128)(2,1)}, u32[]{:S(2)}, u32[]{:S(2)}) async-start(bf16[176,128,128]{2,1,0:T(8,128)(2,1)} %branch_0_fun.5), calls=%async_computation | async-start | bytes 11534336 | tf_op jit(solution)/shard_map/cond/branch_0_fun/all_to_all | solution.py:137
  153.8 98.7 %all-to-all-start.1 = ((bf16[176,128,128]{2,1,0:T(8,128)(2,1)}), bf16[176,128,128]{2,1,0:T(8,128)(2,1)}, u32[]{:S(2)}, u32[]{:S(2)}) async-start(bf16[176,128,128]{2,1,0:T(8,128)(2,1)} %branch_0_fun.8), calls=%async_computation.1 | async-start | bytes 11534336 | tf_op jit(solution)/shard_map/cond/branch_0_fun/all_to_all | solution.py:137
  182.2 162.3 %reduce-scatter.4.cloned.1.call-start = ((), (), s32[]{:S(2)}) async-start(), calls=%async_computation.23 | async-start | bytes 4718592 | tf_op jit(solution)/shard_map/cond/branch_0_fun/reduce_scatter | solution.py:267
  321.2 21.4 %all-to-all-start.5 = ((bf16[16,432,128]{2,1,0:T(8,128)(2,1)}), bf16[16,432,128]{2,1,0:T(8,128)(2,1)S(1)}, u32[]{:S(2)}, u32[]{:S(2)}) async-start(bf16[16,432,128]{2,1,0:T(8,128)(2,1)} %broadcast_in_dim.28), calls=%async_computation.5 | async-start | bytes 3538944 | tf_op jit(solution)/shard_map/cond/branch_0_fun/all_to_all | solution.py:137
  327.7 2.1 collective-permute-start
  327.8 16.8 %copy-start = (f32[16,128,128]{2,1,0:T(8,128)S(1)}, f32[16,128,128]{2,1,0:T(8,128)}, u32[]{:S(2)}) copy-start(f32[16,128,128]{2,1,0:T(8,128)} %get-tuple-element.131) | copy-start | bytes 3145732
  346.0 0.8 copy-start.4
  346.0 1.0 copy-start.6
Sparse Core Ops, SparseCore 0:
  9.8 57.7 all-gather.1
  259.6 66.5 reduce-scatter.3

commit v2 on v1

--- a/solution.py
+++ b/solution.py
@@ -57,9 +57,9 @@
     lax.fori_loop(0, part_ref.shape[0], step, 0, unroll=8)
 
 
-def pack_kernel(code, cot_ref, out_ref):
+def pack_kernel(first, code, cot_ref, out_ref):
     def step(s, carry):
-        out_ref[s] = cot_ref[code[s]]
+        out_ref[s] = cot_ref[code[s], first : first + out_ref.shape[1]]
         return carry
 
     lax.fori_loop(0, out_ref.shape[0], step, 0, unroll=8)
@@ -84,7 +84,7 @@
 
 
 def remote_kernel(
-    offset, block, slot, rows_ref, feat_t_ref, kern_ref, up_ref, in0_ref, w0_ref, in_ref, w_ref
+    offset, block, slot, rows_ref, feat_t_ref, kern_ref, top_ref, low_ref, in0_ref, w0_ref, in_ref, w_ref
 ):
     in_ref[...] = in0_ref[...]
     w_ref[...] = w0_ref[...]
@@ -92,9 +92,8 @@
     def step(q, carry):
         b, k = block[q], offset[q]
         picked = pick_transposed(rows_ref, q, feat_t_ref.shape[2])
-        backward_block(
-            picked, up_ref[slot[q]], feat_t_ref[b], kern_ref[k], in_ref, b, w_ref, k
-        )
+        upstream = jnp.concatenate([top_ref[slot[q]], low_ref[slot[q]]], axis=0)
+        backward_block(picked, upstream, feat_t_ref[b], kern_ref[k], in_ref, b, w_ref, k)
         return carry
 
     lax.fori_loop(0, rows_ref.shape[0], step, 0, unroll=4)
@@ -229,23 +228,29 @@
         codes = code[:, :deep].reshape(slots)
         boxes = [jax.ShapeDtypeStruct((slots, rows, width), BF16)]
 
-        packed = call(pack_kernel, (jnp.maximum(codes, 0),), (column_cot,), boxes)[0]
-        upstream = axis_exchange(packed, PLANE)
+        half = rows // 2
+        halves = [jax.ShapeDtypeStruct((slots, half, width), BF16)]
+        asked = jnp.maximum(codes, 0)
+        packed = call(functools.partial(pack_kernel, 0), (asked,), (column_cot,), halves)[0]
+        top = axis_exchange(packed, PLANE)
+        asked = after(asked, packed)
+        lower = call(functools.partial(pack_kernel, half), (asked,), (column_cot,), halves)[0]
+        low = axis_exchange(after(lower, top), PLANE)
 
         resident, in_sum, w_sum = call(
             local_kernel,
             (pair_offset[:local], pair_block[:local], pair_dest_block[:local]),
-            (after(picks[:local], upstream), feats, feats_t, kern, cot_blocks),
+            (after(picks[:local], low), feats, feats_t, kern, cot_blocks),
             [jax.ShapeDtypeStruct((blocks, rows, width), F32)] + sums,
             flops=4 * local * rows * in_width * (rows + width),
         )
-        placed = call(place_kernel, (place,), (after(parts, packed),), boxes)[0]
-        came = axis_exchange(after(placed, upstream), PLANE)
+        placed = call(place_kernel, (place,), (after(parts, lower),), boxes)[0]
+        came = axis_exchange(after(placed, low), PLANE)
 
         in_sum, w_sum = call(
             remote_kernel,
             (pair_offset[local:], pair_block[local:], place),
-            (picks[local:], feats_t, kern, upstream, in_sum, w_sum),
+            (picks[local:], feats_t, kern, top, low, in_sum, w_sum),
             sums,
             flops=2 * remote * rows * in_width * (rows + width),
         )

time: 355 us -> 340 us (0.958)
  starting transfers between devices: 57.1 us -> 43.4 us
  waiting for transfers between devices: 103 us -> 93.9 us
  blocking collectives: 59.9 us -> 64.6 us
    all_to_all x5 -> x6, starting transfers between devices: 56.9 us -> 43.3 us  [axis_exchange(): return lax.all_to_all(a, axes, split_axis=0, concat_axis=0, tiled=True)]
    all_to_all x5 -> x6, waiting for transfers between devices: 95.8 us -> 86.7 us  [axis_exchange(): return lax.all_to_all(a, axes, split_axis=0, concat_axis=0, tiled=True)]
    all_to_all x3, blocking collectives: 59.9 us -> 64.6 us  [axis_exchange(): return lax.all_to_all(a, axes, split_axis=0, concat_axis=0, tiled=True)]
    pallas_call x6 -> x7, Pallas kernels: 89.2 us -> 92.4 us  [call(): pl.pallas_call(kernel, out_shape=outs, in_specs=[SM] * len(scalars) + [VM...]
  transfers between devices with their start and end apart: 9 -> 10, of which waited for: 7 -> 8; matrix products, arithmetic and copies ran while one was open for 8% -> 8% of each run, Pallas kernels for 22% -> 24%
where the time goes in v2:
time: 340 us; the launch traced here: 339 us
  waiting for transfers between devices  93.9 us (28%)
  Pallas kernels  92.4 us (27%)
  blocking collectives  64.6 us (19%)
  starting transfers between devices  43.4 us (13%)
  other arithmetic  16.1 us (5%)
  between operations  14.9 us (4%)
  local copies, waits for them, and re-layouts  13.8 us (4%)
    pallas_call x7, Pallas kernels, call(): pl.pallas_call(kernel, out_shape=outs, in_specs=[SM] * len(scalars) + [VM...  92.4 us
    all_to_all x6, waiting for transfers between devices, axis_exchange(): return lax.all_to_all(a, axes, split_axis=0, concat_axis=0, tiled=True)  86.7 us
    all_to_all x3, blocking collectives, axis_exchange(): return lax.all_to_all(a, axes, split_axis=0, concat_axis=0, tiled=True)  64.6 us
    all_to_all x6, starting transfers between devices, axis_exchange(): return lax.all_to_all(a, axes, split_axis=0, concat_axis=0, tiled=True)  43.3 us
  transfers between devices with their start and end apart: 10, of which 8 were waited for; matrix products, arithmetic and copies ran while one was open for 8% of the time, Pallas kernels for 24%

profile of v2, /device:TPU:2, one launch (start us, length us, event | category | flops | bytes accessed | tf_op | source)
XLA Modules:
  0.0 339.3 jit_solution(10629704987187482206)
XLA Ops:
  7.3 0.7 all-gather.2.cloned.1.call-update
  8.0 0.7 fusion.4
  8.6 0.8 and_select_fusion.2
  9.6 0.6 fusion.5
  10.4 1.3 concatenate.6
  11.7 7.5 %all-to-all-start.21 = ((s32[16,17,1]{1,2,0:T(1,128)}), s32[16,17,1]{1,2,0:T(1,128)S(1)}, u32[]{:S(2)}, u32[]{:S(2)}) async-start(s32[16,17,1]{1,2,0:T(1,128)} %bitcast.35), calls=%async_computation.24 | async-start | bytes 16384 | tf_op jit(solution)/shard_map/all_to_all | solution.py:136
  19.2 2.2 slice_select_fusion.kern_ref
  21.4 0.6 slice.118.rows_ref
  22.0 0.7 slice.109.offset
  22.7 2.6 all-to-all-done.21
  25.3 0.7 slice_reduce_fusion
  26.0 1.2 reshape.194
  27.2 8.5 %all-to-all-start.22 = ((s32[8,1,1]{2,1,0:T(1,128)}), s32[8,1,1]{2,1,0:T(1,128)S(1)}, u32[]{:S(2)}, u32[]{:S(2)}) async-start(s32[8,1,1]{2,1,0:T(1,128)} %reshape.194), calls=%async_computation.25 | async-start | bytes 8192 | tf_op jit(solution)/shard_map/all_to_all | solution.py:136
  36.3 7.2 %all-to-all-done.22 = s32[8,1,1]{2,1,0:T(1,128)S(1)} async-done(((s32[8,1,1]{2,1,0:T(1,128)}), s32[8,1,1]{2,1,0:T(1,128)S(1)}, u32[]{:S(2)}, u32[]{:S(2)}) %all-to-all-start.22) | async-done | bytes 64 | tf_op jit(solution)/shard_map/all_to_all | solution.py:136
  44.0 16.7 %shard_map.121 = bf16[128,128,128]{2,1,0:T(8,128)(2,1)} custom-call(s32[128]{0:T(128)} %slice.109.offset, s32[128]{0:T(128)} %slice.110.block, s32[128,128]{1,0:T(8,128)} %slice.118.rows_ref, bf16[16,128,256]{2,1,0:T(8,128)(2,1)S(1)} %bitcast.64, bf16[27,256,128]{2,1,0:T(8,128)(2,1)S(1)} %slice_select_fusion.kern_ref), custom_call_target="tpu_custom_call" | custom-call | flops 2147483648 | bytes 7077888 | tf_op jit(solution)/shard_map/pallas_call | solution.py:121
  60.7 0.6 reduce_max.39
  61.3 1.3 fusion.3
  63.2 4.4 %all-gather.2.cloned.1.call-done = bf16[16384,128]{1,0:T(8,128)(2,1)} async-done(((bf16[2048,128]{1,0:T(8,128)(2,1)}), bf16[16384,128]{1,0:T(8,128)(2,1)}) %all-gather.2.cloned.1.call-update) | async-done | bytes 4194320 | tf_op jit(solution)/shard_map/all_gather | solution.py:181
  67.6 263.9 %conditional.4 = (f32[27,256,128]{2,1,0:T(8,128)}, bf16[2048,128]{1,0:T(8,128)(2,1)S(1)}, bf16[2048,128]{1,0:T(8,128)(2,1)S(1)}) conditional(s32[]{:T(128)} %clamp.3, (s32[192]{0:T(256)S(1)}, s32[192]{0:T(256)S(1)}, s32[128]{0:T(128)S(1)}, s32[128]{0:T(128)S(1)}, s32[192,128]{1,0:T(8,128)S(1)}, ...), branch_computations={%region_6.10_spmd, %region_10.14_spmd, %region_14.18_spmd} | conditional | flops 4300082176 | bytes 178428320
  68.3 4.1 %branch_0_fun.6 = bf16[176,64,128]{2,1,0:T(8,128)(2,1)} custom-call(s32[176]{0:T(256)} %get-tuple-element.116.code, bf16[128,128,128]{2,1,0:T(8,128)(2,1)} %bitcast.58), custom_call_target="tpu_custom_call" | custom-call | bytes 7077888 | tf_op jit(solution)/shard_map/cond/branch_0_fun/pallas_call | solution.py:121
  72.4 7.3 %all-to-all-start = ((bf16[176,64,128]{2,1,0:T(8,128)(2,1)}), bf16[176,64,128]{2,1,0:T(8,128)(2,1)}, u32[]{:S(2)}, u32[]{:S(2)}) async-start(bf16[176,64,128]{2,1,0:T(8,128)(2,1)} %branch_0_fun.6), calls=%async_computation | async-start | bytes 5767168 | tf_op jit(solution)/shard_map/cond/branch_0_fun/all_to_all | solution.py:136
  79.7 4.1 %branch_0_fun.7 = bf16[176,64,128]{2,1,0:T(8,128)(2,1)} custom-call(s32[176]{0:T(256)} %get-tuple-element.116.code, bf16[128,128,128]{2,1,0:T(8,128)(2,1)} %bitcast.59), custom_call_target="tpu_custom_call" | custom-call | bytes 7077888 | tf_op jit(solution)/shard_map/cond/branch_0_fun/pallas_call | solution.py:121
  83.8 33.1 %all-to-all-done.top_ref = bf16[176,64,128]{2,1,0:T(8,128)(2,1)} async-done(((bf16[176,64,128]{2,1,0:T(8,128)(2,1)}), bf16[176,64,128]{2,1,0:T(8,128)(2,1)}, u32[]{:S(2)}, u32[]{:S(2)}) %all-to-all-start) | async-done | bytes 2883616 | tf_op jit(solution)/shard_map/cond/branch_0_fun/all_to_all | solution.py:136
  116.9 7.7 %all-to-all-start.1 = ((bf16[176,64,128]{2,1,0:T(8,128)(2,1)}), bf16[176,64,128]{2,1,0:T(8,128)(2,1)}, u32[]{:S(2)}, u32[]{:S(2)}) async-start(bf16[176,64,128]{2,1,0:T(8,128)(2,1)} %branch_0_fun.7), calls=%async_computation.1 | async-start | bytes 5767168 | tf_op jit(solution)/shard_map/cond/branch_0_fun/all_to_all | solution.py:136
  125.2 5.1 %branch_0_fun.10 = bf16[176,128,128]{2,1,0:T(8,128)(2,1)} custom-call(s32[128]{0:T(128)} %multiply_add_fusion.slot, bf16[128,128,128]{2,1,0:T(8,128)(2,1)} %get-tuple-element.126.part_ref), custom_call_target="tpu_custom_call" | custom-call | bytes 9961472 | tf_op jit(solution)/shard_map/cond/branch_0_fun/pallas_call | solution.py:121
  130.3 29.1 %all-to-all-done.1.low_ref = bf16[176,64,128]{2,1,0:T(8,128)(2,1)} async-done(((bf16[176,64,128]{2,1,0:T(8,128)(2,1)}), bf16[176,64,128]{2,1,0:T(8,128)(2,1)}, u32[]{:S(2)}, u32[]{:S(2)}) %all-to-all-start.1) | async-done | bytes 2883616 | tf_op jit(solution)/shard_map/cond/branch_0_fun/all_to_all | solution.py:136
  159.4 7.2 %all-to-all-start.2 = ((bf16[176,128,128]{2,1,0:T(8,128)(2,1)}), bf16[176,128,128]{2,1,0:T(8,128)(2,1)}, u32[]{:S(2)}, u32[]{:S(2)}) async-start(bf16[176,128,128]{2,1,0:T(8,128)(2,1)} %branch_0_fun.10), calls=%async_computation.2 | async-start | bytes 11534336 | tf_op jit(solution)/shard_map/cond/branch_0_fun/all_to_all | solution.py:136
  166.6 0.6 slice.80.rows_ref
  167.2 0.6 slice.75.rows_ref
  168.5 0.6 slice.73.offset
  170.3 1.3 copy.22.feat_t_ref
  172.1 22.6 %branch_0_fun.8 = (f32[16,128,128]{2,1,0:T(8,128)}, f32[16,128,256]{2,1,0:T(8,128)}, f32[27,256,128]{2,1,0:T(8,128)}) custom-call(s32[64]{0:T(128)} %slice.77.offset, s32[64]{0:T(128)} %slice.78.block, s32[64]{0:T(128)} %slice.79.dest, s32[64,128]{1,0:T(8,128)} %slice.80.rows_ref, bf16[16,128,256]{2,1,0:T(8,128)(2,1)S(1)} %bitcast.71, ...), custom_call_target="tpu_custom_call" | custom-call | flops 2147483648 | bytes 11108352 | tf_op jit(solution)/shard_map/cond/branch_0_fun/pallas_call | solution.py:121
  194.7 32.8 %branch_0_fun.9 = (f32[16,128,256]{2,1,0:T(8,128)}, f32[27,256,128]{2,1,0:T(8,128)}) custom-call(s32[128]{0:T(128)} %slice.73.offset, s32[128]{0:T(128)} %slice.74.block, s32[128]{0:T(128)} %multiply_add_fusion.slot, s32[128,128]{1,0:T(8,128)} %slice.75.rows_ref, bf16[16,256,128]{2,1,0:T(8,128)(2,1)} %copy.22.feat_t_ref, ...), custom_call_target="tpu_custom_call" | custom-call | flops 2147483648 | bytes 19922944 | tf_op jit(solution)/shard_map/cond/branch_0_fun/pallas_call | solution.py:121
  227.5 2.3 convert_element_type.96
  229.8 3.6 %all-to-all-done.2.recv_ref = bf16[176,128,128]{2,1,0:T(8,128)(2,1)} async-done(((bf16[176,128,128]{2,1,0:T(8,128)(2,1)}), bf16[176,128,128]{2,1,0:T(8,128)(2,1)}, u32[]{:S(2)}, u32[]{:S(2)}) %all-to-all-start.2) | async-done | bytes 5767200 | tf_op jit(solution)/shard_map/cond/branch_0_fun/all_to_all | solution.py:136
  233.4 7.0 %branch_0_fun.11 = bf16[128,128,128]{2,1,0:T(8,128)(2,1)} custom-call(s32[176]{0:T(256)} %get-tuple-element.130.code, bf16[176,128,128]{2,1,0:T(8,128)(2,1)} %all-to-all-done.2.recv_ref), custom_call_target="tpu_custom_call" | custom-call | bytes 9961472 | tf_op jit(solution)/shard_map/cond/branch_0_fun/pallas_call | solution.py:121
  240.4 28.2 %all_to_all.138 = bf16[16,432,128]{2,1,0:T(8,128)(2,1)S(1)} all-to-all(bf16[16,432,128]{2,1,0:T(8,128)(2,1)S(1)} %bitcast.74), channel_id=1, replica_groups=mesh['x'=4,'y'=4,'z'=8,'chan'=2] {'x','y'}, dimensions={0} | all-to-all | bytes 3538944 | tf_op jit(solution)/shard_map/cond/branch_0_fun/all_to_all | solution.py:136
  268.9 23.4 %all_to_all.139 = bf16[8,64,128]{2,1,0:T(8,128)(2,1)S(1)} all-to-all(bf16[8,64,128]{2,1,0:T(8,128)(2,1)S(1)} %bitcast.89), channel_id=1, replica_groups=mesh['x'=4,'y'=4,'z'=8,'chan'=2] {'z'}, dimensions={0} | all-to-all | bytes 262144 | tf_op jit(solution)/shard_map/cond/branch_0_fun/all_to_all | solution.py:136
  292.3 13.0 %all_to_all.140 = bf16[8,64,128]{2,1,0:T(8,128)(2,1)S(1)} all-to-all(bf16[8,64,128]{2,1,0:T(8,128)(2,1)S(1)} %broadcast_in_dim.27), channel_id=1, replica_groups=mesh['x'=4,'y'=4,'z'=8,'chan'=2] {'z'}, dimensions={0} | all-to-all | bytes 262144 | tf_op jit(solution)/shard_map/cond/branch_0_fun/all_to_all | solution.py:136
  305.4 1.4 broadcast_in_dim.28
  306.8 5.2 %all-to-all-start.6 = ((bf16[16,432,128]{2,1,0:T(8,128)(2,1)}), bf16[16,432,128]{2,1,0:T(8,128)(2,1)S(1)}, u32[]{:S(2)}, u32[]{:S(2)}) async-start(bf16[16,432,128]{2,1,0:T(8,128)(2,1)} %broadcast_in_dim.28), calls=%async_computation.6 | async-start | bytes 3538944 | tf_op jit(solution)/shard_map/cond/branch_0_fun/all_to_all | solution.py:136
  312.0 1.3 dynamic-slice_convert_fusion
  313.4 2.0 collective-permute-done
  315.4 1.5 add_convert_fusion.1
  316.9 11.2 %all-to-all-done.6 = bf16[16,432,128]{2,1,0:T(8,128)(2,1)S(1)} async-done(((bf16[16,432,128]{2,1,0:T(8,128)(2,1)}), bf16[16,432,128]{2,1,0:T(8,128)(2,1)S(1)}, u32[]{:S(2)}, u32[]{:S(2)}) %all-to-all-start.6) | async-done | bytes 1769504 | tf_op jit(solution)/shard_map/cond/branch_0_fun/all_to_all | solution.py:136
  328.1 2.0 convert_multiply_fusion
  330.1 1.2 add_convert_fusion
  331.5 0.8 copy-done.4
  (48 shorter events, 5.7 us)
Async XLA Ops:
  7.2 36.6 %copy-start.3 = (bf16[2048,128]{1,0:T(8,128)(2,1)S(1)}, bf16[2048,128]{1,0:T(8,128)(2,1)}, u32[]{:S(2)}) copy-start(bf16[2048,128]{1,0:T(8,128)(2,1)} %param.13) | copy-start | bytes 1572868
  7.2 14.2 %copy-start.7 = (s32[192,128]{1,0:T(8,128)S(1)}, s32[192,128]{1,0:T(8,128)}, u32[]{:S(2)}) copy-start(s32[192,128]{1,0:T(8,128)} %param.18) | copy-start | bytes 294916
  7.2 14.2 %copy-start.8 = (s32[192,128]{1,0:T(8,128)S(1)}, s32[192,128]{1,0:T(8,128)}, u32[]{:S(2)}) copy-start(s32[192,128]{1,0:T(8,128)} %param.19) | copy-start | bytes 294916
  7.2 14.8 %copy-start.10 = (s32[192]{0:T(256)S(1)}, s32[192]{0:T(256)}, u32[]{:S(2)}) copy-start(s32[192]{0:T(256)} %param.16) | copy-start | bytes 2308
  7.2 28.5 %copy-start.11 = (s32[192]{0:T(256)S(1)}, s32[192]{0:T(256)}, u32[]{:S(2)}) copy-start(s32[192]{0:T(256)} %param.17) | copy-start | bytes 2308
  7.2 60.4 %all-gather.2.cloned.1.call-start = ((), (), s32[]{:S(2)}) async-start(), calls=%async_computation.29 | async-start | bytes 4718592 | tf_op jit(solution)/shard_map/all_gather | solution.py:181
  11.7 13.6 %all-to-all-start.21 = ((s32[16,17,1]{1,2,0:T(1,128)}), s32[16,17,1]{1,2,0:T(1,128)S(1)}, u32[]{:S(2)}, u32[]{:S(2)}) async-start(s32[16,17,1]{1,2,0:T(1,128)} %bitcast.35), calls=%async_computation.24 | async-start | bytes 16384 | tf_op jit(solution)/shard_map/all_to_all | solution.py:136
  19.1 24.6 %collective-permute-start.3 = (bf16[2048,128]{1,0:T(8,128)(2,1)}, bf16[2048,128]{1,0:T(8,128)(2,1)S(1)}, u32[]{:S(2)}, u32[]{:S(2)}) collective-permute-start(bf16[2048,128]{1,0:T(8,128)(2,1)} %param.13), channel_id=1, source_target_pairs={{0,1},{1,0},{2,3},{3,2},{4,5},{5,4},{6,7},{7,6},{8,9},{9,8},{10,11... | collective-permute-start | bytes 1572872 | tf_op jit(solution)/shard_map/ppermute | solution.py:202
  27.2 16.3 %all-to-all-start.22 = ((s32[8,1,1]{2,1,0:T(1,128)}), s32[8,1,1]{2,1,0:T(1,128)S(1)}, u32[]{:S(2)}, u32[]{:S(2)}) async-start(s32[8,1,1]{2,1,0:T(1,128)} %reshape.194), calls=%async_computation.25 | async-start | bytes 8192 | tf_op jit(solution)/shard_map/all_to_all | solution.py:136
  44.0 17.3 %copy-start.12 = (s32[2]{0:T(128)S(1)}, s32[2]{0:T(128)}, u32[]{:S(2)}) copy-start(s32[2]{0:T(128)} %constant.99.clone) | copy-start | bytes 28
  44.0 23.7 %copy-start.5 = (bf16[2048,128]{1,0:T(8,128)(2,1)S(1)}, bf16[2048,128]{1,0:T(8,128)(2,1)}, u32[]{:S(2)}) copy-start(bf16[2048,128]{1,0:T(8,128)(2,1)} %param.15) | copy-start | bytes 1572868
  44.0 23.7 %copy-start.9 = (s32[192]{0:T(256)S(1)}, s32[192]{0:T(256)}, u32[]{:S(2)}) copy-start(s32[192]{0:T(256)} %param.20) | copy-start | bytes 2308
  72.4 44.5 %all-to-all-start = ((bf16[176,64,128]{2,1,0:T(8,128)(2,1)}), bf16[176,64,128]{2,1,0:T(8,128)(2,1)}, u32[]{:S(2)}, u32[]{:S(2)}) async-start(bf16[176,64,128]{2,1,0:T(8,128)(2,1)} %branch_0_fun.6), calls=%async_computation | async-start | bytes 5767168 | tf_op jit(solution)/shard_map/cond/branch_0_fun/all_to_all | solution.py:136
  116.9 42.4 %all-to-all-start.1 = ((bf16[176,64,128]{2,1,0:T(8,128)(2,1)}), bf16[176,64,128]{2,1,0:T(8,128)(2,1)}, u32[]{:S(2)}, u32[]{:S(2)}) async-start(bf16[176,64,128]{2,1,0:T(8,128)(2,1)} %branch_0_fun.7), calls=%async_computation.1 | async-start | bytes 5767168 | tf_op jit(solution)/shard_map/cond/branch_0_fun/all_to_all | solution.py:136
  159.4 74.0 %all-to-all-start.2 = ((bf16[176,128,128]{2,1,0:T(8,128)(2,1)}), bf16[176,128,128]{2,1,0:T(8,128)(2,1)}, u32[]{:S(2)}, u32[]{:S(2)}) async-start(bf16[176,128,128]{2,1,0:T(8,128)(2,1)} %branch_0_fun.10), calls=%async_computation.2 | async-start | bytes 11534336 | tf_op jit(solution)/shard_map/cond/branch_0_fun/all_to_all | solution.py:136
  166.6 163.5 %reduce-scatter.4.cloned.1.call-start = ((), (), s32[]{:S(2)}) async-start(), calls=%async_computation.26 | async-start | bytes 4718592 | tf_op jit(solution)/shard_map/cond/branch_0_fun/reduce_scatter | solution.py:272
  306.8 21.3 %all-to-all-start.6 = ((bf16[16,432,128]{2,1,0:T(8,128)(2,1)}), bf16[16,432,128]{2,1,0:T(8,128)(2,1)S(1)}, u32[]{:S(2)}, u32[]{:S(2)}) async-start(bf16[16,432,128]{2,1,0:T(8,128)(2,1)} %broadcast_in_dim.28), calls=%async_computation.6 | async-start | bytes 3538944 | tf_op jit(solution)/shard_map/cond/branch_0_fun/all_to_all | solution.py:136
  313.2 2.1 collective-permute-start
  313.3 16.7 %copy-start = (f32[16,128,128]{2,1,0:T(8,128)S(1)}, f32[16,128,128]{2,1,0:T(8,128)}, u32[]{:S(2)}) copy-start(f32[16,128,128]{2,1,0:T(8,128)} %get-tuple-element.133) | copy-start | bytes 3145732
  331.5 0.8 copy-start.4
  331.5 1.0 copy-start.6
Sparse Core Ops, SparseCore 0:
  9.8 57.7 all-gather.1
  240.6 71.4 reduce-scatter.3
